TPU v7x, 32 devices: a whole 2x2x4 slice. The times are simulated.
32 devices in a mesh: groups: 2 (over y), col: 4 (over z), row: 2 (over x), rhs: 2 (over core).
Axes of the slice: x: 2, y: 2, z: 4, core: 2. Of those that a mesh axis runs over, the one named last changes fastest.
Arguments:
- prev_panel: float32 [4, 2048, 4096], P(None, 'row', 'col'), may hold values from -0.09375 to 0.09375
- lower_panel: float32 [3, 2048, 3, 2048], P(None, 'row', None, 'col'), may hold values from -0.125 to 0.125
- solved_prev: float32 [4096, 1024], P('col', ('groups', 'rhs')), parts along dimension 1, may hold values from -6 to 6
- right_block: float32 [8, 2048, 512], P('groups', 'row', 'rhs'), parts along dimension 0, may hold values from -6 to 6
- block_inverse: float32 [4, 2048, 2048], P(None, 'col', 'row'), may hold values from -1 to 1, as said below
Outputs:
- solved: float32 [8, 2048, 512], P('groups', 'col', 'rhs'), parts along dimension 0
There are 2 independent parts, one for each index of `groups`. A program takes and returns all parts, laid end to end along the dimension named above; an argument that names none is the same for every part. Nothing has to cross between parts.
Inputs may be any that keep to these rules, and one draw needn't show every extreme that they name: Each block_inverse[k] is lower triangular with diagonal entries from 0.5 to 1.
All inputs are finite; a program needn't handle non-finite values.
Results may differ from a plain program's by a relative error of at most 0.0001.
Values sent between devices are 32-bit elements; how exact they have to be, the bound alone decides.
A program may use at most 128 MiB of HBM per device.

v0:
```python
import jax
import jax.numpy as jnp
from jax import lax
from jax.sharding import PartitionSpec as P


def product(left, right):
    return jnp.dot(left, right, precision=lax.Precision.HIGHEST, preferred_element_type=jnp.float32)


def column_sum(partial_value):
    return lax.psum(partial_value, "col")


def local(prev_panel, lower_panel, solved_prev, right_block, block_inverse):
    blocks = prev_panel.shape[0]
    solved = []
    for block in range(blocks):
        partial_value = product(prev_panel[block], solved_prev)
        for earlier in range(block):
            partial_value = partial_value + product(
                lower_panel[block - 1, :, earlier, :], solved[earlier]
            )
        total = column_sum(partial_value)
        residual = right_block[block] - total
        piece = product(block_inverse[block], residual)
        result = lax.psum(piece, "row")
        solved.append(result)
    return jnp.stack(solved)


def solution(mesh):
    return jax.shard_map(
        local,
        mesh=mesh,
        in_specs=(
            P(None, "row", "col"),
            P(None, "row", None, "col"),
            P("col", ("groups", "rhs")),
            P("groups", "row", "rhs"),
            P(None, "col", "row"),
        ),
        out_specs=P("groups", "col", "rhs"),
        check_vma=False,
    )
```

profile of v0, /device:TPU:0, one launch (start us, length us, event | category | flops | bytes accessed | tf_op | source)
XLA Modules:
  0.0 405.6 jit_solution(14568761899108600092)
XLA Ops:
  6.5 1.2 copy-done
  7.8 6.6 %fusion.6 = f32[1024,256]{1,0:T(8,128)} fusion(f32[1024,256]{1,0:T(8,128)S(1)} %copy-done, f32[4,1024,1024]{2,1,0:T(8,128)} %param.5), kind=kOutput, calls=%fused_computation.6 | convolution fusion | flops 3221225472 | bytes 6291456 | tf_op jit(solution)/shard_map/dot_general | solution.py:8
  14.4 0.0 all-reduce.11.cloned.1.call-start
  14.4 54.7 %all-reduce.9.cloned.1.call-done = f32[1024,256]{1,0:T(8,128)} async-done(((f32[1024,256]{1,0:T(8,128)}), f32[1024,256]{1,0:T(8,128)}) %all-reduce.9.cloned.1.call-update) | async-done | bytes 1048592 | tf_op jit(solution)/shard_map/psum | solution.py:12
  69.1 6.6 %fusion.78 = f32[512,256]{0,1:T(8,128)} fusion(f32[4,512,1024]{2,1,0:T(8,128)} %param.9, f32[1024,256]{1,0:T(8,128)} %all-reduce.9.cloned.1.call-done, f32[4,1024,256]{2,1,0:T(8,128)} %param.8), kind=kOutput, calls=%fused_computation.55 | convolution fusion | flops 1610874880 | bytes 4718592 | tf_op jit(solution)/shard_map/dot_general | solution.py:8
  75.7 0.2 all-reduce.13.cloned.1.call-start
  76.0 27.8 %all-reduce.11.cloned.1.call-done = f32[512,256]{0,1:T(8,128)} async-done(((f32[512,256]{0,1:T(8,128)}), f32[512,256]{0,1:T(8,128)}) %all-reduce.11.cloned.1.call-update) | async-done | bytes 524304 | tf_op jit(solution)/shard_map/psum | solution.py:27
  103.8 3.6 fusion.42
  107.4 6.6 %fusion.60 = f32[1024,256]{1,0:T(8,128)} fusion(f32[1024,256]{1,0:T(8,128)S(1)} %fusion.42, f32[1024,256]{1,0:T(8,128)S(1)} %copy-done, f32[4,1024,1024]{2,1,0:T(8,128)} %param.5), kind=kOutput, calls=%fused_computation.49 | convolution fusion | flops 3221487616 | bytes 7340032 | tf_op jit(solution)/shard_map/dot_general | solution.py:8
  114.1 0.0 all-reduce.15.cloned.1.call-start
  114.1 52.0 %all-reduce.13.cloned.1.call-done = f32[1024,256]{1,0:T(8,128)} async-done(((f32[1024,256]{1,0:T(8,128)}), f32[1024,256]{1,0:T(8,128)}) %all-reduce.13.cloned.1.call-update) | async-done | bytes 1048592 | tf_op jit(solution)/shard_map/psum | solution.py:12
  166.1 6.6 %fusion.81 = f32[512,256]{0,1:T(8,128)} fusion(f32[4,512,1024]{2,1,0:T(8,128)} %param.9, f32[1024,256]{1,0:T(8,128)} %all-reduce.13.cloned.1.call-done, f32[4,1024,256]{2,1,0:T(8,128)} %param.8), kind=kOutput, calls=%fused_computation.56 | convolution fusion | flops 1610874880 | bytes 4718592 | tf_op jit(solution)/shard_map/dot_general | solution.py:8
  172.7 0.3 all-reduce.17.cloned.1.call-start
  173.0 3.4 fusion.45
  176.4 24.4 %all-reduce.15.cloned.1.call-done = f32[512,256]{0,1:T(8,128)} async-done(((f32[512,256]{0,1:T(8,128)}), f32[512,256]{0,1:T(8,128)}) %all-reduce.15.cloned.1.call-update) | async-done | bytes 524304 | tf_op jit(solution)/shard_map/psum | solution.py:27
  200.8 3.6 fusion.48
  204.4 6.6 %fusion.66 = f32[1024,256]{1,0:T(8,128)} fusion(f32[1024,256]{1,0:T(8,128)S(1)} %fusion.48, f32[1024,256]{1,0:T(8,128)S(1)} %fusion.45, f32[1024,256]{1,0:T(8,128)S(1)} %copy-done, f32[4,1024,1024]{2,1,0:T(8,128)} %param.5), kind=kOutput, calls=%fused_computation.51 | convolution fusion | flops 3221749760 | bytes 8388608 | tf_op jit(solution)/shard_map/dot_general | solution.py:8
  211.0 0.0 all-reduce.19.cloned.1.call-start
  211.1 52.0 %all-reduce.17.cloned.1.call-done = f32[1024,256]{1,0:T(8,128)} async-done(((f32[1024,256]{1,0:T(8,128)}), f32[1024,256]{1,0:T(8,128)}) %all-reduce.17.cloned.1.call-update) | async-done | bytes 1048592 | tf_op jit(solution)/shard_map/psum | solution.py:12
  263.1 6.6 %fusion.84 = f32[512,256]{0,1:T(8,128)} fusion(f32[4,512,1024]{2,1,0:T(8,128)} %param.9, f32[1024,256]{1,0:T(8,128)} %all-reduce.17.cloned.1.call-done, f32[4,1024,256]{2,1,0:T(8,128)} %param.8), kind=kOutput, calls=%fused_computation.57 | convolution fusion | flops 1610874880 | bytes 4718592 | tf_op jit(solution)/shard_map/dot_general | solution.py:8
  269.7 0.3 all-reduce.21.cloned.1.call-start
  270.0 3.4 fusion.51
  273.4 4.6 %fusion.54 = f32[1024,256]{1,0:T(8,128)} fusion(f32[512,256]{0,1:T(8,128)S(1)} %copy-done.2, f32[3,1024,3,512]{3,1,2,0:T(8,128)} %param.6), kind=kOutput, calls=%fused_computation.47 | convolution fusion | flops 1610612736 | bytes 3670016 | tf_op jit(solution)/shard_map/dot_general | solution.py:8
  278.0 19.7 %all-reduce.19.cloned.1.call-done = f32[512,256]{0,1:T(8,128)} async-done(((f32[512,256]{0,1:T(8,128)}), f32[512,256]{0,1:T(8,128)}) %all-reduce.19.cloned.1.call-update) | async-done | bytes 524304 | tf_op jit(solution)/shard_map/psum | solution.py:27
  297.7 3.6 fusion.57
  301.4 6.6 %fusion.75 = f32[1024,256]{1,0:T(8,128)} fusion(f32[1024,256]{1,0:T(8,128)S(1)} %fusion.57, f32[1024,256]{1,0:T(8,128)S(1)} %copy-done.3, f32[1024,256]{1,0:T(8,128)S(1)} %fusion.51, f32[1024,256]{1,0:T(8,128)S(1)} %copy-done, f32[4,1024,1024]{2,1,0:T(8,128)} %param.5), kind=kOutput, calls=%fused_computation.54 | convolution fusion | flops 3222011904 | bytes 9437184 | tf_op jit(solution)/shard_map/dot_general | solution.py:8
  308.0 0.3 all-reduce.23.cloned.1.call-start
  308.4 51.7 %all-reduce.21.cloned.1.call-done = f32[1024,256]{1,0:T(8,128)} async-done(((f32[1024,256]{1,0:T(8,128)}), f32[1024,256]{1,0:T(8,128)}) %all-reduce.21.cloned.1.call-update) | async-done | bytes 1048592 | tf_op jit(solution)/shard_map/psum | solution.py:12
  360.1 6.6 %fusion.87 = f32[1,512,256]{1,2,0:T(8,128)} fusion(f32[4,512,1024]{2,1,0:T(8,128)} %param.9, f32[1024,256]{1,0:T(8,128)} %all-reduce.21.cloned.1.call-done, f32[4,1024,256]{2,1,0:T(8,128)} %param.8), kind=kOutput, calls=%fused_computation.58 | convolution fusion | flops 1610874880 | bytes 4718592 | tf_op jit(solution)/shard_map/dot_general | solution.py:8
  366.7 28.1 %all-reduce.23.cloned.1.call-done = f32[1,512,256]{1,2,0:T(8,128)} async-done(((f32[1,512,256]{1,2,0:T(8,128)}), f32[1,512,256]{1,2,0:T(8,128)}) %all-reduce.23.cloned.1.call-update) | async-done | bytes 524304 | tf_op jit(solution)/shard_map/psum | solution.py:27
  394.7 1.7 pad_maximum_fusion
  396.4 1.8 copy.6
  (16 shorter events, 0.1 us)
Async XLA Ops:
  6.5 1.2 copy-start
  6.5 62.6 %all-reduce.9.cloned.1.call-start = ((), (), s32[]{:S(2)}) async-start(), calls=%async_computation | async-start | bytes 2097152 | tf_op jit(solution)/shard_map/psum | solution.py:12
  14.4 89.5 %all-reduce.11.cloned.1.call-start = ((), (), s32[]{:S(2)}) async-start(), calls=%async_computation.1 | async-start | bytes 1048576 | tf_op jit(solution)/shard_map/psum | solution.py:27
  75.7 90.4 %all-reduce.13.cloned.1.call-start = ((), (), s32[]{:S(2)}) async-start(), calls=%async_computation.2 | async-start | bytes 2097152 | tf_op jit(solution)/shard_map/psum | solution.py:12
  114.0 59.0 %copy-start.1 = (f32[512,256]{0,1:T(8,128)S(1)}, f32[512,256]{0,1:T(8,128)}, u32[]{:S(2)}) copy-start(f32[512,256]{0,1:T(8,128)} %all-reduce.11.cloned.1.call-done) | copy-start | bytes 1572868
  114.1 86.7 %all-reduce.15.cloned.1.call-start = ((), (), s32[]{:S(2)}) async-start(), calls=%async_computation.3 | async-start | bytes 1048576 | tf_op jit(solution)/shard_map/psum | solution.py:27
  172.7 90.3 %all-reduce.17.cloned.1.call-start = ((), (), s32[]{:S(2)}) async-start(), calls=%async_computation.4 | async-start | bytes 2097152 | tf_op jit(solution)/shard_map/psum | solution.py:12
  211.0 62.4 %copy-start.2 = (f32[512,256]{0,1:T(8,128)S(1)}, f32[512,256]{0,1:T(8,128)}, u32[]{:S(2)}) copy-start(f32[512,256]{0,1:T(8,128)} %all-reduce.15.cloned.1.call-done) | copy-start | bytes 1572868
  211.0 86.7 %all-reduce.19.cloned.1.call-start = ((), (), s32[]{:S(2)}) async-start(), calls=%async_computation.5 | async-start | bytes 1048576 | tf_op jit(solution)/shard_map/psum | solution.py:27
  269.7 90.4 %all-reduce.21.cloned.1.call-start = ((), (), s32[]{:S(2)}) async-start(), calls=%async_computation.6 | async-start | bytes 2097152 | tf_op jit(solution)/shard_map/psum | solution.py:12
  278.0 23.4 %copy-start.3 = (f32[1024,256]{1,0:T(8,128)S(1)}, f32[1024,256]{1,0:T(8,128)}, u32[]{:S(2)}) copy-start(f32[1024,256]{1,0:T(8,128)} %fusion.54) | copy-start | bytes 3145732
  308.0 86.7 %all-reduce.23.cloned.1.call-start = ((), (), s32[]{:S(2)}) async-start(), calls=%async_computation.7 | async-start | bytes 1048576 | tf_op jit(solution)/shard_map/psum | solution.py:27
Sparse Core Ops, SparseCore 0:
  14.5 54.6 all-reduce.8
  75.9 27.8 all-reduce.10
  114.2 51.8 all-reduce.12
  172.8 27.8 all-reduce.14
  211.1 51.8 all-reduce.16
  269.8 27.8 all-reduce.18
  308.2 51.8 all-reduce.20
  366.8 27.8 all-reduce.22
where the time goes:
time: 412 us; the launch traced here: 406 us
  waiting for transfers between devices  311 us (75%)
  matrix products  75 us (18%)
  between operations  14.1 us (3%)
    psum x4, waiting for transfers between devices, column_sum(): return lax.psum(partial_value, 'col')  210 us
    psum x4, waiting for transfers between devices, local(): result = lax.psum(piece, 'row')  100 us
    dot_general x14, matrix products, product(): jnp.dot(left, right, precision=lax.Precision.HIGHEST, preferred_element_t...  75 us
  transfers between devices with their start and end apart: 8, of which 8 were waited for; matrix products, arithmetic and copies ran while one was open for 3% of the time, Pallas kernels for 0%

commit v1 on v0

v1 whole, which is shorter than its diff:
```python
import functools

import jax
import jax.numpy as jnp
from jax import lax
from jax.experimental import pallas as pl
from jax.experimental.pallas import tpu as pltpu
from jax.sharding import PartitionSpec as P

F32, BF16 = jnp.float32, jnp.bfloat16
MESH = pl.DeviceIdType.MESH


def split(value):
    high = value.astype(BF16)
    return high, (value - high.astype(F32)).astype(BF16)


def product(left, both):
    high, low = split(left)
    n = both.shape[1] // 2
    wide = jnp.dot(high, both, preferred_element_type=F32)
    return wide[:, :n] + wide[:, n:] + jnp.dot(low, both[:, :n], preferred_element_type=F32)


def kernel(
    C, R, S,
    prev_hbm, lower_hbm, sprev_hbm, right_hbm, inv_hbm, out_ref,
    prev, lower, sprev, right, inv, sprev_both, part, from_l, from_r, to_l, to_r,
    xsend, xrecv, solved, acc,
    prev_sem, lower_sem, sprev_sem, right_sem, inv_sem,
    send_r, recv_l, send_l, recv_r, xs_sem, xr_sem,
):
    blocks, NR, _ = prev.shape
    NC = out_ref.shape[1]
    MH = part.shape[-1]
    CR = NR // S
    steps = 2 * blocks
    c, r = lax.axis_index("col"), lax.axis_index("row")
    has_l, has_r = c > 0, c < C - 1
    left, right_of = jnp.maximum(c - 1, 0), jnp.minimum(c + 1, C - 1)

    def rows(i):
        return pl.ds(pl.multiple_of(i * CR, CR), CR)

    def tri(k, j):
        return lax.div(k * (k - 1), 2) + j

    def load_prev(k):
        return pltpu.make_async_copy(prev_hbm.at[k], prev.at[k], prev_sem.at[k])

    def load_right(k):
        return pltpu.make_async_copy(right_hbm.at[k], right.at[k], right_sem.at[k])

    def load_inv(k, i):
        return pltpu.make_async_copy(inv_hbm.at[k, :, rows(i)], inv.at[k, i], inv_sem.at[k, i])

    def load_lower(k, j):
        return pltpu.make_async_copy(lower_hbm.at[k - 1, j], lower.at[tri(k, j)], lower_sem.at[tri(k, j)])

    def loop(n, body, start=0):
        lax.fori_loop(start, n, lambda i, _: (body(i), 0)[1], 0)

    load_sprev = pltpu.make_async_copy(sprev_hbm, sprev, sprev_sem)
    load_sprev.start()
    load_prev(0).start()
    load_right(0).start()
    loop(S, lambda i: load_inv(0, i).start())

    barrier = pltpu.get_barrier_semaphore()

    @pl.when(has_l)
    def _():
        pl.semaphore_signal(barrier, inc=1, device_id={"col": left}, device_id_type=MESH)

    @pl.when(has_r)
    def _():
        pl.semaphore_signal(barrier, inc=1, device_id={"col": right_of}, device_id_type=MESH)

    for d in range(1, R):
        pl.semaphore_signal(barrier, inc=1, device_id={"row": lax.rem(r + d, R)}, device_id_type=MESH)

    @pl.when(jnp.logical_not(has_l))
    def _():
        from_l[...] = jnp.zeros_like(from_l)

    @pl.when(jnp.logical_not(has_r))
    def _():
        from_r[...] = jnp.zeros_like(from_r)

    def push_right(p, i):
        return pltpu.make_async_remote_copy(
            src_ref=to_r.at[p, i], dst_ref=from_l.at[p, i],
            send_sem=send_r.at[p, i], recv_sem=recv_l.at[p, i],
            device_id={"col": right_of}, device_id_type=MESH)

    def push_left(p, i):
        return pltpu.make_async_remote_copy(
            src_ref=to_l.at[p, i], dst_ref=from_r.at[p, i],
            send_sem=send_l.at[p, i], recv_sem=recv_r.at[p, i],
            device_id={"col": left}, device_id_type=MESH)

    def push_x(slot, d):
        return pltpu.make_async_remote_copy(
            src_ref=xsend.at[slot], dst_ref=xrecv.at[slot, d - 1],
            send_sem=xs_sem.at[slot, d - 1], recv_sem=xr_sem.at[slot, d - 1],
            device_id={"row": lax.rem(r + d, R)}, device_id_type=MESH)

    def base(k, i):
        high, low = split(prev[k, rows(i), :])
        m = sprev_both.shape[1] // 2
        s_hi, s_lo = sprev_both[:, :m], sprev_both[:, m:]
        a = jnp.dot(high, s_hi, preferred_element_type=F32)
        a = a + jnp.dot(high, s_lo, preferred_element_type=F32)
        a = a + jnp.dot(low, s_hi, preferred_element_type=F32)
        value = jnp.where(has_l, 0.0, right[k, rows(i), :]) - a
        kp = lax.rem(k, 2)
        part[kp, 0, i] = value[:, :MH]
        part[kp, 1, i] = value[:, MH:]

    load_sprev.wait()
    m = sprev.shape[1]
    s_hi, s_lo = split(sprev[...])
    sprev_both[:, :m] = s_hi
    sprev_both[:, m:] = s_lo
    load_prev(0).wait()
    load_right(0).wait()
    pl.semaphore_wait(barrier, has_l.astype(jnp.int32) + has_r.astype(jnp.int32) + (R - 1))

    def consume(t):
        slot, k, h = lax.rem(t, 4), lax.div(t, 2), lax.rem(t, 2)
        total = xsend[slot]
        for d in range(1, R):
            push_x(slot, d).wait_recv()
            total = total + xrecv[slot, d - 1]
        for d in range(1, R):
            push_x(slot, d).wait_send()
        solved[k, h, :, :MH], solved[k, h, :, MH:] = split(total)

        @pl.when(h == 0)
        def _():
            out_ref[k, :, :MH] = total

        @pl.when(h == 1)
        def _():
            out_ref[k, :, MH:] = total

    def drain(p):
        def body(i):
            @pl.when(has_r)
            def _():
                push_right(p, i).wait_send()

            @pl.when(has_l)
            def _():
                push_left(p, i).wait_send()

        loop(S, body)

    def step(t):
        k, h = lax.div(t, 2), lax.rem(t, 2)
        kp, p, nk = lax.rem(k, 2), h, jnp.minimum(k + 1, blocks - 1)
        more = k < blocks - 1
        fresh = jnp.logical_and(h == 0, more)

        @pl.when(fresh)
        def _():
            load_prev(nk).start()
            load_right(nk).start()
            loop(k + 1, lambda j: load_lower(nk, j).start())
            loop(S, lambda i: load_inv(nk, i).start())

        def own(i):
            @pl.when(t == 0)
            def _():
                base(0, i)

            @pl.when(k > 0)
            def _():
                part[kp, h, i] -= product(lower[tri(k, k - 1), rows(i), :], solved[jnp.maximum(k - 1, 0), h])

            @pl.when(jnp.logical_not(has_l))
            def _():
                to_r[p, i] = part[kp, h, i]
                push_right(p, i).start()

            @pl.when(jnp.logical_not(has_r))
            def _():
                to_l[p, i] = part[kp, h, i]
                push_left(p, i).start()

        loop(S, own)

        @pl.when(fresh)
        def _():
            load_prev(nk).wait()
            load_right(nk).wait()
            loop(k + 1, lambda j: load_lower(nk, j).wait())

        def pass_right(i):
            @pl.when(has_l)
            def _():
                push_right(p, i).wait_recv()

                @pl.when(has_r)
                def _():
                    to_r[p, i] = from_l[p, i] + part[kp, h, i]
                    push_right(p, i).start()

        def pass_left(i):
            @pl.when(has_r)
            def _():
                push_left(p, i).wait_recv()

                @pl.when(has_l)
                def _():
                    to_l[p, i] = from_r[p, i] + part[kp, h, i]
                    push_left(p, i).start()

        def chunk(i):
            first = c < C // 2

            @pl.when(first)
            def _():
                pass_right(i)
                pass_left(i)

            @pl.when(jnp.logical_not(first))
            def _():
                pass_left(i)
                pass_right(i)

            @pl.when(h == 0)
            def _():
                load_inv(k, i).wait()

            high, low = split(from_l[p, i] + part[kp, h, i] + from_r[p, i])
            piece = product(inv[k, i], jnp.concatenate([high, low], axis=1))

            @pl.when(i == 0)
            def _():
                acc[...] = piece

            @pl.when(i > 0)
            def _():
                acc[...] += piece

            @pl.when(fresh)
            def _():
                base(nk, i)

            @pl.when(more)
            def _():
                def older(j):
                    part[1 - kp, h, i] -= product(lower[tri(nk, j), rows(i), :], solved[j, h])

                loop(k, older)

        loop(S, chunk)
        slot = lax.rem(t, 4)
        xsend[slot] = acc[...]
        for d in range(1, R):
            push_x(slot, d).start()

        @pl.when(t > 0)
        def _():
            consume(t - 1)
            drain(1 - p)

    loop(steps, step)
    consume(steps - 1)
    drain((steps - 1) % 2)


def local(C, R, prev_panel, lower_panel, solved_prev, right_block, block_inverse):
    blocks, NR, KP = prev_panel.shape
    M = solved_prev.shape[1]
    NC, MH = block_inverse.shape[1], M // 2
    S = max(1, min(4, NR // 128))
    CR = NR // S
    pairs = blocks * (blocks - 1) // 2
    dma = pltpu.SemaphoreType.DMA
    wide = pltpu.VMEM((2, S, CR, MH), F32)
    return pl.pallas_call(
        functools.partial(kernel, C, R, S),
        out_shape=jax.ShapeDtypeStruct((blocks, NC, M), F32),
        in_specs=[pl.BlockSpec(memory_space=pl.ANY)] * 5,
        out_specs=pl.BlockSpec(memory_space=pltpu.VMEM),
        scratch_shapes=[
            pltpu.VMEM((blocks, NR, KP), F32),
            pltpu.VMEM((pairs, NR, NC), F32),
            pltpu.VMEM((KP, M), F32),
            pltpu.VMEM((blocks, NR, M), F32),
            pltpu.VMEM((blocks, S, NC, CR), F32),
            pltpu.VMEM((KP, 2 * M), BF16),
            pltpu.VMEM((2, 2, S, CR, MH), F32),
            wide, wide, wide, wide,
            pltpu.VMEM((4, NC, MH), F32),
            pltpu.VMEM((4, max(R - 1, 1), NC, MH), F32),
            pltpu.VMEM((blocks, 2, NC, 2 * MH), BF16),
            pltpu.VMEM((NC, MH), F32),
            dma((blocks,)), dma((pairs,)), dma, dma((blocks,)), dma((blocks, S)),
            dma((2, S)), dma((2, S)), dma((2, S)), dma((2, S)),
            dma((4, max(R - 1, 1))), dma((4, max(R - 1, 1))),
        ],
        compiler_params=pltpu.CompilerParams(
            collective_id=0, has_side_effects=True, vmem_limit_bytes=63 * 2**20),
    )(prev_panel, jnp.transpose(lower_panel, (0, 2, 1, 3)), solved_prev, right_block, block_inverse)


def solution(mesh):
    return jax.shard_map(
        functools.partial(local, mesh.shape["col"], mesh.shape["row"]),
        mesh=mesh,
        in_specs=(
            P(None, "row", "col"),
            P(None, "row", None, "col"),
            P("col", ("groups", "rhs")),
            P("groups", "row", "rhs"),
            P(None, "col", "row"),
        ),
        out_specs=P("groups", "col", "rhs"),
        check_vma=False,
    )
```

time: 412 us -> 249 us (0.60); the launches traced: 406 us -> 249 us
  waiting for transfers between devices: 311 us -> 0 us
  Pallas kernels: 0 us -> 246 us
  matrix products: 75 us -> 0 us
  between operations: 14.1 us -> 0.01 us
    psum x8 -> x0, waiting for transfers between devices: 310 us -> none  [the longest x4 210 us: column_sum(): return lax.psum(partial_value, 'col')]
    pallas_call x0 -> x1, Pallas kernels: none -> 246 us  [local(): pl.pallas_call(functools.partial(kernel, C, R, S), out_shape=jax.ShapeDty...]
    dot_general x14 -> x0, matrix products: 75 us -> none  [product(): jnp.dot(left, right, precision=lax.Precision.HIGHEST, preferred_element_t...]
  transfers between devices with their start and end apart: 8 -> 0, of which waited for: 8 -> 0; matrix products, arithmetic and copies ran while one was open for 3% -> 0% of each run, Pallas kernels for 0% -> 0%
where the time goes in v1:
time: 249 us
  Pallas kernels  246 us (99%)
  local copies, waits for them, and re-layouts  3.05 us (1%)
    pallas_call x1, Pallas kernels, local(): pl.pallas_call(functools.partial(kernel, C, R, S), out_shape=jax.ShapeDty...  246 us

profile of v1, /device:TPU:0, one launch (start us, length us, event | category | flops | bytes accessed | tf_op | source)
XLA Modules:
  0.0 248.8 jit_solution(10811189153734654220)
XLA Ops:
  0.0 245.8 %shard_map.55 = f32[4,512,256]{2,1,0:T(8,128)} custom-call(f32[4,1024,1024]{2,1,0:T(8,128)} %prev_hbm.1, f32[3,3,1024,512]{3,2,1,0:T(8,128)} %bitcast.1, f32[1024,256]{1,0:T(8,128)} %sprev_hbm.1, f32[4,1024,256]{2,1,0:T(8,128)} %right_hbm.1, f32[4,512,1024]{2,1,0:T(8,128)} %inv_hbm.1), custom_call_target="tpu_custom_call" | custom-call | tf_op jit(solution)/shard_map/pallas_call | solution.py:284
  245.8 3.0 %copy.7 = f32[4,512,256]{2,1,0:T(8,128)} copy(f32[4,512,256]{2,1,0:T(8,128)} %shard_map.55) | data formatting | bytes 4194304

commit v2 on v1

--- a/solution.py
+++ b/solution.py
@@ -24,7 +24,7 @@
 
 
 def kernel(
-    C, R, S,
+    C, R, S, LAG, INJ,
     prev_hbm, lower_hbm, sprev_hbm, right_hbm, inv_hbm, out_ref,
     prev, lower, sprev, right, inv, sprev_both, part, from_l, from_r, to_l, to_r,
     xsend, xrecv, solved, acc,
@@ -157,11 +157,29 @@
 
         loop(S, body)
 
+    def own(t, i):
+        k, h = lax.div(t, 2), lax.rem(t, 2)
+        kp, last = lax.rem(k, 2), jnp.maximum(k - 1, 0)
+
+        @pl.when(k > 0)
+        def _():
+            part[kp, h, i] -= product(lower[tri(k, last), rows(i), :], solved[last, h])
+
+        @pl.when(jnp.logical_not(has_l))
+        def _():
+            to_r[h, i] = part[kp, h, i]
+            push_right(h, i).start()
+
+        @pl.when(jnp.logical_not(has_r))
+        def _():
+            to_l[h, i] = part[kp, h, i]
+            push_left(h, i).start()
+
     def step(t):
-        k, h = lax.div(t, 2), lax.rem(t, 2)
-        kp, p, nk = lax.rem(k, 2), h, jnp.minimum(k + 1, blocks - 1)
+        k, p = lax.div(t, 2), lax.rem(t, 2)
+        kp, nk = lax.rem(k, 2), jnp.minimum(k + 1, blocks - 1)
         more = k < blocks - 1
-        fresh = jnp.logical_and(h == 0, more)
+        fresh = jnp.logical_and(p == 0, more)
 
         @pl.when(fresh)
         def _():
@@ -170,33 +188,6 @@
             loop(k + 1, lambda j: load_lower(nk, j).start())
             loop(S, lambda i: load_inv(nk, i).start())
 
-        def own(i):
-            @pl.when(t == 0)
-            def _():
-                base(0, i)
-
-            @pl.when(k > 0)
-            def _():
-                part[kp, h, i] -= product(lower[tri(k, k - 1), rows(i), :], solved[jnp.maximum(k - 1, 0), h])
-
-            @pl.when(jnp.logical_not(has_l))
-            def _():
-                to_r[p, i] = part[kp, h, i]
-                push_right(p, i).start()
-
-            @pl.when(jnp.logical_not(has_r))
-            def _():
-                to_l[p, i] = part[kp, h, i]
-                push_left(p, i).start()
-
-        loop(S, own)
-
-        @pl.when(fresh)
-        def _():
-            load_prev(nk).wait()
-            load_right(nk).wait()
-            loop(k + 1, lambda j: load_lower(nk, j).wait())
-
         def pass_right(i):
             @pl.when(has_l)
             def _():
@@ -204,7 +195,7 @@
 
                 @pl.when(has_r)
                 def _():
-                    to_r[p, i] = from_l[p, i] + part[kp, h, i]
+                    to_r[p, i] = from_l[p, i] + part[kp, p, i]
                     push_right(p, i).start()
 
         def pass_left(i):
@@ -214,27 +205,26 @@
 
                 @pl.when(has_l)
                 def _():
-                    to_l[p, i] = from_r[p, i] + part[kp, h, i]
+                    to_l[p, i] = from_r[p, i] + part[kp, p, i]
                     push_left(p, i).start()
 
-        def chunk(i):
-            first = c < C // 2
-
-            @pl.when(first)
+        first = c < C // 2
+
+        def either(flag, i):
+            @pl.when(flag)
             def _():
                 pass_right(i)
+
+            @pl.when(jnp.logical_not(flag))
+            def _():
                 pass_left(i)
 
-            @pl.when(jnp.logical_not(first))
-            def _():
-                pass_left(i)
-                pass_right(i)
-
-            @pl.when(h == 0)
+        def use(i):
+            @pl.when(p == 0)
             def _():
                 load_inv(k, i).wait()
 
-            high, low = split(from_l[p, i] + part[kp, h, i] + from_r[p, i])
+            high, low = split(from_l[p, i] + part[kp, p, i] + from_r[p, i])
             piece = product(inv[k, i], jnp.concatenate([high, low], axis=1))
 
             @pl.when(i == 0)
@@ -245,28 +235,60 @@
             def _():
                 acc[...] += piece
 
+        def ahead(i):
             @pl.when(fresh)
             def _():
+                @pl.when(i == 0)
+                def _():
+                    load_prev(nk).wait()
+                    load_right(nk).wait()
+                    loop(k + 1, lambda j: load_lower(nk, j).wait())
+
                 base(nk, i)
 
             @pl.when(more)
             def _():
                 def older(j):
-                    part[1 - kp, h, i] -= product(lower[tri(nk, j), rows(i), :], solved[j, h])
+                    part[1 - kp, p, i] -= product(lower[tri(nk, j), rows(i), :], solved[j, p])
 
                 loop(k, older)
 
-        loop(S, chunk)
+        def turn(n):
+            @pl.when(n < S)
+            def _():
+                either(first, n)
+
+            @pl.when(n >= LAG)
+            def _():
+                either(jnp.logical_not(first), n - LAG)
+
+            @pl.when(n == INJ)
+            def _():
+                @pl.when(t > 0)
+                def _():
+                    consume(t - 1)
+                    drain(1 - p)
+
+                @pl.when(t < steps - 1)
+                def _():
+                    loop(S, lambda i: own(t + 1, i))
+
+            @pl.when(n >= LAG)
+            def _():
+                use(n - LAG)
+                ahead(n - LAG)
+
+        loop(S + LAG, turn)
         slot = lax.rem(t, 4)
         xsend[slot] = acc[...]
         for d in range(1, R):
             push_x(slot, d).start()
 
-        @pl.when(t > 0)
-        def _():
-            consume(t - 1)
-            drain(1 - p)
-
+    def begin(i):
+        base(0, i)
+        own(0, i)
+
+    loop(S, begin)
     loop(steps, step)
     consume(steps - 1)
     drain((steps - 1) % 2)
@@ -276,13 +298,15 @@
     blocks, NR, KP = prev_panel.shape
     M = solved_prev.shape[1]
     NC, MH = block_inverse.shape[1], M // 2
-    S = max(1, min(4, NR // 128))
+    S = max(1, min(8, NR // 128))
+    LAG = min(2, S - 1)
+    INJ = max(LAG, S * 5 // 8)
     CR = NR // S
     pairs = blocks * (blocks - 1) // 2
     dma = pltpu.SemaphoreType.DMA
     wide = pltpu.VMEM((2, S, CR, MH), F32)
     return pl.pallas_call(
-        functools.partial(kernel, C, R, S),
+        functools.partial(kernel, C, R, S, LAG, INJ),
         out_shape=jax.ShapeDtypeStruct((blocks, NC, M), F32),
         in_specs=[pl.BlockSpec(memory_space=pl.ANY)] * 5,
         out_specs=pl.BlockSpec(memory_space=pltpu.VMEM),

time: 249 us -> 152 us (0.61)
  Pallas kernels: 246 us -> 149 us
    pallas_call x1, Pallas kernels: 246 us -> 149 us  [local(): pl.pallas_call(functools.partial(kernel, C, R, S, LAG, INJ), out_shape=ja...]
where the time goes in v2:
time: 152 us
  Pallas kernels  149 us (98%)
  local copies, waits for them, and re-layouts  3.05 us (2%)
    pallas_call x1, Pallas kernels, local(): pl.pallas_call(functools.partial(kernel, C, R, S, LAG, INJ), out_shape=ja...  149 us
    unnamed x1, local copies, waits for them, and re-layouts  3.05 us

profile of v2, /device:TPU:0, one launch (start us, length us, event | category | flops | bytes accessed | tf_op | source)
XLA Modules:
  0.0 152.0 jit_solution(5572938108984752489)
XLA Ops:
  0.0 148.9 %shard_map.55 = f32[4,512,256]{2,1,0:T(8,128)} custom-call(f32[4,1024,1024]{2,1,0:T(8,128)} %prev_hbm.1, f32[3,3,1024,512]{3,2,1,0:T(8,128)} %bitcast.1, f32[1024,256]{1,0:T(8,128)} %sprev_hbm.1, f32[4,1024,256]{2,1,0:T(8,128)} %right_hbm.1, f32[4,512,1024]{2,1,0:T(8,128)} %inv_hbm.1), custom_call_target="tpu_custom_call" | custom-call | tf_op jit(solution)/shard_map/pallas_call | solution.py:308
  148.9 3.0 %copy.7 = f32[4,512,256]{2,1,0:T(8,128)} copy(f32[4,512,256]{2,1,0:T(8,128)} %shard_map.55) | data formatting | bytes 4194304

commit v3 on v2

--- a/solution.py
+++ b/solution.py
@@ -24,7 +24,7 @@
 
 
 def kernel(
-    C, R, S, LAG, INJ,
+    C, R, S, G, LAG, INJ,
     prev_hbm, lower_hbm, sprev_hbm, right_hbm, inv_hbm, out_ref,
     prev, lower, sprev, right, inv, sprev_both, part, from_l, from_r, to_l, to_r,
     xsend, xrecv, solved, acc,
@@ -35,13 +35,17 @@
     NC = out_ref.shape[1]
     MH = part.shape[-1]
     CR = NR // S
+    Q, QR = S // G, CR * G
     steps = 2 * blocks
     c, r = lax.axis_index("col"), lax.axis_index("row")
     has_l, has_r = c > 0, c < C - 1
     left, right_of = jnp.maximum(c - 1, 0), jnp.minimum(c + 1, C - 1)
 
-    def rows(i):
-        return pl.ds(pl.multiple_of(i * CR, CR), CR)
+    def rows(q):
+        return pl.ds(pl.multiple_of(q * QR, QR), QR)
+
+    def group(q):
+        return pl.ds(q * G, G)
 
     def tri(k, j):
         return lax.div(k * (k - 1), 2) + j
@@ -65,7 +69,7 @@
     load_sprev.start()
     load_prev(0).start()
     load_right(0).start()
-    loop(S, lambda i: load_inv(0, i).start())
+    loop(Q, lambda q: load_inv(0, q).start())
 
     barrier = pltpu.get_barrier_semaphore()
 
@@ -115,8 +119,8 @@
         a = a + jnp.dot(low, s_hi, preferred_element_type=F32)
         value = jnp.where(has_l, 0.0, right[k, rows(i), :]) - a
         kp = lax.rem(k, 2)
-        part[kp, 0, i] = value[:, :MH]
-        part[kp, 1, i] = value[:, MH:]
+        part[kp, 0, group(i)] = value[:, :MH].reshape(G, CR, MH)
+        part[kp, 1, group(i)] = value[:, MH:].reshape(G, CR, MH)
 
     load_sprev.wait()
     m = sprev.shape[1]
@@ -157,23 +161,26 @@
 
         loop(S, body)
 
-    def own(t, i):
+    def own(t, q):
         k, h = lax.div(t, 2), lax.rem(t, 2)
         kp, last = lax.rem(k, 2), jnp.maximum(k - 1, 0)
 
         @pl.when(k > 0)
         def _():
-            part[kp, h, i] -= product(lower[tri(k, last), rows(i), :], solved[last, h])
+            less = product(lower[tri(k, last), rows(q), :], solved[last, h])
+            part[kp, h, group(q)] -= less.reshape(G, CR, MH)
 
         @pl.when(jnp.logical_not(has_l))
         def _():
-            to_r[h, i] = part[kp, h, i]
-            push_right(h, i).start()
+            to_r[h, group(q)] = part[kp, h, group(q)]
+            for g in range(G):
+                push_right(h, q * G + g).start()
 
         @pl.when(jnp.logical_not(has_r))
         def _():
-            to_l[h, i] = part[kp, h, i]
-            push_left(h, i).start()
+            to_l[h, group(q)] = part[kp, h, group(q)]
+            for g in range(G):
+                push_left(h, q * G + g).start()
 
     def step(t):
         k, p = lax.div(t, 2), lax.rem(t, 2)
@@ -186,7 +193,7 @@
             load_prev(nk).start()
             load_right(nk).start()
             loop(k + 1, lambda j: load_lower(nk, j).start())
-            loop(S, lambda i: load_inv(nk, i).start())
+            loop(Q, lambda q: load_inv(nk, q).start())
 
         def pass_right(i):
             @pl.when(has_l)
@@ -224,7 +231,8 @@
             def _():
                 load_inv(k, i).wait()
 
-            high, low = split(from_l[p, i] + part[kp, p, i] + from_r[p, i])
+            total = from_l[p, group(i)] + part[kp, p, group(i)] + from_r[p, group(i)]
+            high, low = split(total.reshape(QR, MH))
             piece = product(inv[k, i], jnp.concatenate([high, low], axis=1))
 
             @pl.when(i == 0)
@@ -249,7 +257,8 @@
             @pl.when(more)
             def _():
                 def older(j):
-                    part[1 - kp, p, i] -= product(lower[tri(nk, j), rows(i), :], solved[j, p])
+                    less = product(lower[tri(nk, j), rows(i), :], solved[j, p])
+                    part[1 - kp, p, group(i)] -= less.reshape(G, CR, MH)
 
                 loop(k, older)
 
@@ -271,12 +280,13 @@
 
                 @pl.when(t < steps - 1)
                 def _():
-                    loop(S, lambda i: own(t + 1, i))
-
-            @pl.when(n >= LAG)
-            def _():
-                use(n - LAG)
-                ahead(n - LAG)
+                    loop(Q, lambda q: own(t + 1, q))
+
+            @pl.when(jnp.logical_and(n >= LAG, lax.rem(n - LAG + 1, G) == 0))
+            def _():
+                q = lax.div(n - LAG, G)
+                use(q)
+                ahead(q)
 
         loop(S + LAG, turn)
         slot = lax.rem(t, 4)
@@ -288,7 +298,7 @@
         base(0, i)
         own(0, i)
 
-    loop(S, begin)
+    loop(Q, begin)
     loop(steps, step)
     consume(steps - 1)
     drain((steps - 1) % 2)
@@ -300,13 +310,14 @@
     NC, MH = block_inverse.shape[1], M // 2
     S = max(1, min(8, NR // 128))
     LAG = min(2, S - 1)
-    INJ = max(LAG, S * 5 // 8)
+    INJ = max(LAG, S * 4 // 8)
+    G = 2 if S % 2 == 0 else 1
     CR = NR // S
     pairs = blocks * (blocks - 1) // 2
     dma = pltpu.SemaphoreType.DMA
     wide = pltpu.VMEM((2, S, CR, MH), F32)
     return pl.pallas_call(
-        functools.partial(kernel, C, R, S, LAG, INJ),
+        functools.partial(kernel, C, R, S, G, LAG, INJ),
         out_shape=jax.ShapeDtypeStruct((blocks, NC, M), F32),
         in_specs=[pl.BlockSpec(memory_space=pl.ANY)] * 5,
         out_specs=pl.BlockSpec(memory_space=pltpu.VMEM),
@@ -315,7 +326,7 @@
             pltpu.VMEM((pairs, NR, NC), F32),
             pltpu.VMEM((KP, M), F32),
             pltpu.VMEM((blocks, NR, M), F32),
-            pltpu.VMEM((blocks, S, NC, CR), F32),
+            pltpu.VMEM((blocks, S // G, NC, CR * G), F32),
             pltpu.VMEM((KP, 2 * M), BF16),
             pltpu.VMEM((2, 2, S, CR, MH), F32),
             wide, wide, wide, wide,
@@ -323,7 +334,7 @@
             pltpu.VMEM((4, max(R - 1, 1), NC, MH), F32),
             pltpu.VMEM((blocks, 2, NC, 2 * MH), BF16),
             pltpu.VMEM((NC, MH), F32),
-            dma((blocks,)), dma((pairs,)), dma, dma((blocks,)), dma((blocks, S)),
+            dma((blocks,)), dma((pairs,)), dma, dma((blocks,)), dma((blocks, S // G)),
             dma((2, S)), dma((2, S)), dma((2, S)), dma((2, S)),
             dma((4, max(R - 1, 1))), dma((4, max(R - 1, 1))),
         ],

time: 152 us -> 143 us (0.941)
  Pallas kernels: 149 us -> 140 us
    pallas_call x1, Pallas kernels: 149 us -> 140 us  [local(): pl.pallas_call(functools.partial(kernel, C, R, S, G, LAG, INJ), out_shape...]
where the time goes in v3:
time: 143 us
  Pallas kernels  140 us (98%)
  local copies, waits for them, and re-layouts  3.05 us (2%)
    pallas_call x1, Pallas kernels, local(): pl.pallas_call(functools.partial(kernel, C, R, S, G, LAG, INJ), out_shape...  140 us
    unnamed x1, local copies, waits for them, and re-layouts  3.05 us

profile of v3, /device:TPU:0, one launch (start us, length us, event | category | flops | bytes accessed | tf_op | source)
XLA Modules:
  0.0 142.9 jit_solution(10718623201640685701)
XLA Ops:
  0.0 139.9 %shard_map.55 = f32[4,512,256]{2,1,0:T(8,128)} custom-call(f32[4,1024,1024]{2,1,0:T(8,128)} %prev_hbm.1, f32[3,3,1024,512]{3,2,1,0:T(8,128)} %bitcast.1, f32[1024,256]{1,0:T(8,128)} %sprev_hbm.1, f32[4,1024,256]{2,1,0:T(8,128)} %right_hbm.1, f32[4,512,1024]{2,1,0:T(8,128)} %inv_hbm.1), custom_call_target="tpu_custom_call" | custom-call | tf_op jit(solution)/shard_map/pallas_call | solution.py:319
  139.9 3.0 %copy.7 = f32[4,512,256]{2,1,0:T(8,128)} copy(f32[4,512,256]{2,1,0:T(8,128)} %shard_map.55) | data formatting | bytes 4194304
